TPU v7x, 128 devices: a whole 4x4x4 slice. The times are simulated.
128 devices in a mesh: ctx: 16 (over y_lo, x, core), exp: 8 (over y_hi, z).
Axes of the slice: x: 4, y: 4 (y_hi: 2, y_lo: 2; y = y_hi * 2 + y_lo), z: 4, core: 2. Of those that a mesh axis runs over, the one named last changes fastest.
Arguments:
- queries: bfloat16 [2048, 3072], P('ctx', 'exp'), may hold values from -8 to 8
- keys: bfloat16 [2048, 1024], P('ctx', 'exp'), may hold values from -8 to 8
- values: bfloat16 [2048, 1024], P('ctx', 'exp'), may hold values from -6 to 6
- norm_gain: float32 [3072], replicated, may hold values from 0.1 to 1.9
- routes: int32 [2048, 2], P(('ctx', 'exp')), may hold values from 0 to 7, all different within a row; in each aligned block of 16 rows (0 to 15, 16 to 31, ...) at most 6 rows name the same one
- route_scores: float32 [2048, 2], P(('ctx', 'exp')), may hold values from -8 to 8
- cotangent: bfloat16 [2048, 3072], P(('ctx', 'exp')), may hold values from -6 to 6
- w_gate: bfloat16 [8, 3072, 8192], P('exp', None, 'ctx'), may hold values from -0.109375 to 0.109375
- w_up: bfloat16 [8, 3072, 8192], P('exp', None, 'ctx'), may hold values from -0.109375 to 0.109375
- w_down: bfloat16 [8, 8192, 3072], P('exp', 'ctx'), may hold values from -0.0625 to 0.0625
Outputs:
- mixed: bfloat16 [2048, 3072], P(('ctx', 'exp'))
- grad_input: bfloat16 [2048, 3072], P(('ctx', 'exp'))
- grad_gate: bfloat16 [8, 3072, 8192], P('exp', None, 'ctx')
- grad_up: bfloat16 [8, 3072, 8192], P('exp', None, 'ctx')
- grad_down: bfloat16 [8, 8192, 3072], P('exp', 'ctx')
Inputs may be any that keep to these rules, and one draw needn't show every extreme that they name: `routes`: each row names two different experts. Within each aligned block of 16 rows (the rows of one device) no expert is named by more than 6 rows, a bound that some block reaches.
All inputs are finite; a program needn't handle non-finite values.
Results may differ from a plain program's by a relative error of at most 0.018.
Values may be sent and summed in bfloat16 or wider, within the bound.
A program may use at most 128 MiB of HBM per device.

v0:
```python
import jax
import jax.numpy as jnp
from jax import lax
from jax.sharding import PartitionSpec as P

norm_eps = 1e-05
masked_value = -1e30


def shifted(block, axis, distance):
    devices = range(lax.axis_size(axis))
    route = [(i - distance, i) for i in devices if i - distance in devices]
    return lax.ppermute(block, axis, route)


def heads_first(query_local, group, head):
    count = query_local.shape[0]
    return query_local.reshape(count, group, head).transpose(1, 0, 2).reshape(group * count, head)


def attend_piece(state, query_flat, query_pos, piece, start, head):
    running_max, running_sum, accum = state
    key_part = piece[:, :head]
    value_part = piece[:, head:].astype(jnp.float32)
    scores = lax.dot_general(
        query_flat, key_part, (((1,), (1,)), ((), ())), preferred_element_type=jnp.float32
    ) * head ** (-0.5)
    key_pos = start + jnp.arange(piece.shape[0], dtype=jnp.int32)
    allowed = key_pos[None, :] <= query_pos[:, None]
    scores = jnp.where(allowed, scores, masked_value)
    new_max = jnp.maximum(running_max, jnp.max(scores, axis=1))
    weights = jnp.where(allowed, jnp.exp(scores - new_max[:, None]), 0.0)
    factor = jnp.exp(running_max - new_max)
    new_sum = running_sum * factor + jnp.sum(weights, axis=1)
    product = jnp.dot(
        weights, value_part, precision=lax.Precision.HIGHEST, preferred_element_type=jnp.float32
    )
    new_accum = accum * factor[:, None] + product
    return (new_max, new_sum, new_accum)


def local(queries, keys, values, norm_gain, routes, route_scores, cotangent, w_gate, w_up, w_down):
    n_ctx = lax.axis_size("ctx")
    n_exp = lax.axis_size("exp")
    head = keys.shape[1]
    group = queries.shape[1] // head
    tok_ctx = queries.shape[0]
    ctx_index = lax.axis_index("ctx")
    query_flat = heads_first(queries, group, head)
    query_pos = ctx_index * tok_ctx + jnp.tile(jnp.arange(tok_ctx, dtype=jnp.int32), group)
    key_values = jnp.concatenate([keys, values], axis=1)
    query_rows = query_flat.shape[0]
    initial = (
        jnp.full((query_rows,), masked_value, jnp.float32),
        jnp.zeros((query_rows,), jnp.float32),
        jnp.zeros((query_rows, head), jnp.float32),
    )
    first = attend_piece(initial, query_flat, query_pos, key_values, ctx_index * tok_ctx, head)

    def cycle_step(step, carry):
        state, current = carry
        current = shifted(current, "ctx", 1)
        source = (ctx_index - step) % n_ctx
        state = attend_piece(state, query_flat, query_pos, current, source * tok_ctx, head)
        return (state, current)

    state, _ = lax.fori_loop(1, n_ctx, cycle_step, (first, key_values))
    running_max, running_sum, accum = state
    attended = accum / running_sum[:, None]
    attended = (
        attended.reshape(group, tok_ctx, head)
        .transpose(1, 0, 2)
        .reshape(tok_ctx, group * head)
        .astype(jnp.bfloat16)
    )
    features = lax.all_to_all(attended, "exp", split_axis=0, concat_axis=1, tiled=True)
    feats = features.astype(jnp.float32)
    inv_rms = lax.rsqrt(jnp.mean(feats * feats, axis=1) + norm_eps)
    normed = (feats * inv_rms[:, None] * norm_gain[None, :]).astype(jnp.bfloat16)
    tok_dev = normed.shape[0]
    width = normed.shape[1]
    capacity = 3 * tok_dev // n_exp
    slots = n_exp * capacity
    flat_routes = routes.reshape(-1)
    onehot = (flat_routes[:, None] == jnp.arange(n_exp, dtype=jnp.int32)[None, :]).astype(jnp.int32)
    ranks = jnp.sum((jnp.cumsum(onehot, axis=0) - onehot) * onehot, axis=1)
    target = flat_routes * capacity + ranks
    placed = (jnp.arange(slots, dtype=jnp.int32)[:, None] == target[None, :]).astype(jnp.float32)
    place_tokens = placed.reshape(slots, tok_dev, 2).sum(axis=2)
    probs = jax.nn.softmax(route_scores, axis=1)
    mixing = (placed * probs.reshape(-1)[None, :]).reshape(slots, tok_dev, 2).sum(axis=2)
    send = jnp.dot(
        place_tokens.astype(jnp.bfloat16), normed, preferred_element_type=jnp.float32
    ).astype(jnp.bfloat16)
    arrived = lax.all_to_all(
        send.reshape(n_exp, capacity, width), "exp", split_axis=0, concat_axis=0, tiled=True
    ).reshape(slots, width)
    expert_in = lax.all_gather(arrived, "ctx", axis=0, tiled=True)
    gate_w = w_gate[0]
    up_w = w_up[0]
    down_w = w_down[0]
    gate_pre = jnp.dot(expert_in, gate_w, preferred_element_type=jnp.float32)
    up_pre = jnp.dot(expert_in, up_w, preferred_element_type=jnp.float32)
    hidden = (jax.nn.silu(gate_pre) * up_pre).astype(jnp.bfloat16)
    expert_out = lax.psum_scatter(
        jnp.dot(hidden, down_w, preferred_element_type=jnp.float32).astype(jnp.bfloat16),
        "ctx",
        scatter_dimension=0,
        tiled=True,
    )
    returned = lax.all_to_all(
        expert_out.reshape(n_exp, capacity, width), "exp", split_axis=0, concat_axis=0, tiled=True
    ).reshape(slots, width)
    mixed = lax.dot_general(
        mixing,
        returned.astype(jnp.float32),
        (((0,), (0,)), ((), ())),
        precision=lax.Precision.HIGHEST,
    ).astype(jnp.bfloat16)
    grad_slots = jnp.dot(
        mixing, cotangent.astype(jnp.float32), precision=lax.Precision.HIGHEST
    ).astype(jnp.bfloat16)
    grad_arrived = lax.all_to_all(
        grad_slots.reshape(n_exp, capacity, width), "exp", split_axis=0, concat_axis=0, tiled=True
    ).reshape(slots, width)
    grad_out, rows_in = (
        lax.all_gather(grad_arrived, "ctx", axis=0, tiled=True),
        lax.all_gather(arrived, "ctx", axis=0, tiled=True),
    )
    grad_hidden = lax.dot_general(
        grad_out, down_w, (((1,), (1,)), ((), ())), preferred_element_type=jnp.float32
    )
    grad_down = lax.dot_general(
        hidden, grad_out, (((0,), (0,)), ((), ())), preferred_element_type=jnp.float32
    ).astype(jnp.bfloat16)
    sig = jax.nn.sigmoid(gate_pre)
    grad_up_pre = (grad_hidden * (gate_pre * sig)).astype(jnp.bfloat16)
    grad_gate_pre = (grad_hidden * up_pre * sig * (1.0 + gate_pre * (1.0 - sig))).astype(
        jnp.bfloat16
    )
    grad_gate = lax.dot_general(
        rows_in, grad_gate_pre, (((0,), (0,)), ((), ())), preferred_element_type=jnp.float32
    ).astype(jnp.bfloat16)
    grad_upw = lax.dot_general(
        rows_in, grad_up_pre, (((0,), (0,)), ((), ())), preferred_element_type=jnp.float32
    ).astype(jnp.bfloat16)
    term = lax.dot_general(
        grad_gate_pre, gate_w, (((1,), (1,)), ((), ())), preferred_element_type=jnp.float32
    )
    grad_summed = lax.psum_scatter(
        (
            term
            + lax.dot_general(
                grad_up_pre, up_w, (((1,), (1,)), ((), ())), preferred_element_type=jnp.float32
            )
        ).astype(jnp.bfloat16),
        "ctx",
        scatter_dimension=0,
        tiled=True,
    )
    grad_back = lax.all_to_all(
        grad_summed.reshape(n_exp, capacity, width), "exp", split_axis=0, concat_axis=0, tiled=True
    ).reshape(slots, width)
    grad_normed = lax.dot_general(
        place_tokens,
        grad_back.astype(jnp.float32),
        (((0,), (0,)), ((), ())),
        precision=lax.Precision.HIGHEST,
    )
    weighted = grad_normed * norm_gain[None, :]
    inner = jnp.mean(weighted * feats, axis=1)
    grad_input = (inv_rms[:, None] * weighted - feats * (inv_rms**3 * inner)[:, None]).astype(
        jnp.bfloat16
    )
    return (mixed, grad_input, grad_gate[None], grad_upw[None], grad_down[None])


def solution(mesh):
    placed = (
        P("ctx", "exp"),
        P("ctx", "exp"),
        P("ctx", "exp"),
        P(),
        P(("ctx", "exp"), None),
        P(("ctx", "exp"), None),
        P(("ctx", "exp"), None),
        P("exp", None, "ctx"),
        P("exp", None, "ctx"),
        P("exp", "ctx", None),
    )
    return jax.shard_map(
        local,
        mesh=mesh,
        in_specs=placed,
        out_specs=(
            P(("ctx", "exp"), None),
            P(("ctx", "exp"), None),
            P("exp", None, "ctx"),
            P("exp", None, "ctx"),
            P("exp", "ctx", None),
        ),
        check_vma=False,
    )
```

profile of v0, /device:TPU:16, one launch (start us, length us, event | category | flops | bytes accessed | tf_op | source)
XLA Modules:
  0.0 441.2 jit_solution(11982174086630426389)
XLA Ops:
  12.2 109.1 %while.22 = (s32[]{:T(128)}, f32[384]{0:T(512)S(1)}, f32[384]{0:T(512)S(1)}, f32[384,128]{1,0:T(8,128)S(1)}, bf16[128,256]{1,0:T(8,128)(2,1)}, /*index=5*/s32[]{...) while((s32[]{:T(128)}, f32[384]{0:T(512)S(1)}, ...), condition=%wide.region_11.12_spmd.clone, body=%wide.region_8.11_spmd.clone.sunk | while | flops 88720656 | bytes 1575218 | solution.py:67
  23.3 4.7 %collective-permute-start = (bf16[128,256]{1,0:T(8,128)(2,1)}, bf16[128,256]{1,0:T(8,128)(2,1)S(1)}, u32[]{:S(2)}, u32[]{:S(2)}) collective-permute-start(bf16[128,256]{1,0:T(8,128)(2,1)} %get-tuple-element.331), channel_id=1, source_target_pairs={{0,8},{8,16},{16,24},{24,32},{32,40},{40,48},{48,56},{56,64},{64,7... | collective-permute-start | bytes 196616 | tf_op jit(solution)/shard_map/while/body/eval_jaxpr/ppermute | solution.py:13
  30.5 4.7 %collective-permute-start = (bf16[128,256]{1,0:T(8,128)(2,1)}, bf16[128,256]{1,0:T(8,128)(2,1)S(1)}, u32[]{:S(2)}, u32[]{:S(2)}) collective-permute-start(bf16[128,256]{1,0:T(8,128)(2,1)} %get-tuple-element.331), channel_id=1, source_target_pairs={{0,8},{8,16},{16,24},{24,32},{32,40},{40,48},{48,56},{56,64},{64,7... | collective-permute-start | bytes 196616 | tf_op jit(solution)/shard_map/while/body/eval_jaxpr/ppermute | solution.py:13
  37.8 4.7 %collective-permute-start = (bf16[128,256]{1,0:T(8,128)(2,1)}, bf16[128,256]{1,0:T(8,128)(2,1)S(1)}, u32[]{:S(2)}, u32[]{:S(2)}) collective-permute-start(bf16[128,256]{1,0:T(8,128)(2,1)} %get-tuple-element.331), channel_id=1, source_target_pairs={{0,8},{8,16},{16,24},{24,32},{32,40},{40,48},{48,56},{56,64},{64,7... | collective-permute-start | bytes 196616 | tf_op jit(solution)/shard_map/while/body/eval_jaxpr/ppermute | solution.py:13
  45.0 4.7 %collective-permute-start = (bf16[128,256]{1,0:T(8,128)(2,1)}, bf16[128,256]{1,0:T(8,128)(2,1)S(1)}, u32[]{:S(2)}, u32[]{:S(2)}) collective-permute-start(bf16[128,256]{1,0:T(8,128)(2,1)} %get-tuple-element.331), channel_id=1, source_target_pairs={{0,8},{8,16},{16,24},{24,32},{32,40},{40,48},{48,56},{56,64},{64,7... | collective-permute-start | bytes 196616 | tf_op jit(solution)/shard_map/while/body/eval_jaxpr/ppermute | solution.py:13
  52.3 4.7 %collective-permute-start = (bf16[128,256]{1,0:T(8,128)(2,1)}, bf16[128,256]{1,0:T(8,128)(2,1)S(1)}, u32[]{:S(2)}, u32[]{:S(2)}) collective-permute-start(bf16[128,256]{1,0:T(8,128)(2,1)} %get-tuple-element.331), channel_id=1, source_target_pairs={{0,8},{8,16},{16,24},{24,32},{32,40},{40,48},{48,56},{56,64},{64,7... | collective-permute-start | bytes 196616 | tf_op jit(solution)/shard_map/while/body/eval_jaxpr/ppermute | solution.py:13
  59.5 4.7 %collective-permute-start = (bf16[128,256]{1,0:T(8,128)(2,1)}, bf16[128,256]{1,0:T(8,128)(2,1)S(1)}, u32[]{:S(2)}, u32[]{:S(2)}) collective-permute-start(bf16[128,256]{1,0:T(8,128)(2,1)} %get-tuple-element.331), channel_id=1, source_target_pairs={{0,8},{8,16},{16,24},{24,32},{32,40},{40,48},{48,56},{56,64},{64,7... | collective-permute-start | bytes 196616 | tf_op jit(solution)/shard_map/while/body/eval_jaxpr/ppermute | solution.py:13
  66.7 4.7 %collective-permute-start = (bf16[128,256]{1,0:T(8,128)(2,1)}, bf16[128,256]{1,0:T(8,128)(2,1)S(1)}, u32[]{:S(2)}, u32[]{:S(2)}) collective-permute-start(bf16[128,256]{1,0:T(8,128)(2,1)} %get-tuple-element.331), channel_id=1, source_target_pairs={{0,8},{8,16},{16,24},{24,32},{32,40},{40,48},{48,56},{56,64},{64,7... | collective-permute-start | bytes 196616 | tf_op jit(solution)/shard_map/while/body/eval_jaxpr/ppermute | solution.py:13
  74.0 4.7 %collective-permute-start = (bf16[128,256]{1,0:T(8,128)(2,1)}, bf16[128,256]{1,0:T(8,128)(2,1)S(1)}, u32[]{:S(2)}, u32[]{:S(2)}) collective-permute-start(bf16[128,256]{1,0:T(8,128)(2,1)} %get-tuple-element.331), channel_id=1, source_target_pairs={{0,8},{8,16},{16,24},{24,32},{32,40},{40,48},{48,56},{56,64},{64,7... | collective-permute-start | bytes 196616 | tf_op jit(solution)/shard_map/while/body/eval_jaxpr/ppermute | solution.py:13
  81.2 4.7 %collective-permute-start = (bf16[128,256]{1,0:T(8,128)(2,1)}, bf16[128,256]{1,0:T(8,128)(2,1)S(1)}, u32[]{:S(2)}, u32[]{:S(2)}) collective-permute-start(bf16[128,256]{1,0:T(8,128)(2,1)} %get-tuple-element.331), channel_id=1, source_target_pairs={{0,8},{8,16},{16,24},{24,32},{32,40},{40,48},{48,56},{56,64},{64,7... | collective-permute-start | bytes 196616 | tf_op jit(solution)/shard_map/while/body/eval_jaxpr/ppermute | solution.py:13
  88.5 4.7 %collective-permute-start = (bf16[128,256]{1,0:T(8,128)(2,1)}, bf16[128,256]{1,0:T(8,128)(2,1)S(1)}, u32[]{:S(2)}, u32[]{:S(2)}) collective-permute-start(bf16[128,256]{1,0:T(8,128)(2,1)} %get-tuple-element.331), channel_id=1, source_target_pairs={{0,8},{8,16},{16,24},{24,32},{32,40},{40,48},{48,56},{56,64},{64,7... | collective-permute-start | bytes 196616 | tf_op jit(solution)/shard_map/while/body/eval_jaxpr/ppermute | solution.py:13
  95.7 4.7 %collective-permute-start = (bf16[128,256]{1,0:T(8,128)(2,1)}, bf16[128,256]{1,0:T(8,128)(2,1)S(1)}, u32[]{:S(2)}, u32[]{:S(2)}) collective-permute-start(bf16[128,256]{1,0:T(8,128)(2,1)} %get-tuple-element.331), channel_id=1, source_target_pairs={{0,8},{8,16},{16,24},{24,32},{32,40},{40,48},{48,56},{56,64},{64,7... | collective-permute-start | bytes 196616 | tf_op jit(solution)/shard_map/while/body/eval_jaxpr/ppermute | solution.py:13
  103.0 6.5 %collective-permute-start = (bf16[128,256]{1,0:T(8,128)(2,1)}, bf16[128,256]{1,0:T(8,128)(2,1)S(1)}, u32[]{:S(2)}, u32[]{:S(2)}) collective-permute-start(bf16[128,256]{1,0:T(8,128)(2,1)} %get-tuple-element.331), channel_id=1, source_target_pairs={{0,8},{8,16},{16,24},{24,32},{32,40},{40,48},{48,56},{56,64},{64,7... | collective-permute-start | bytes 196616 | tf_op jit(solution)/shard_map/while/body/eval_jaxpr/ppermute | solution.py:13
  112.0 6.8 %collective-permute-start = (bf16[128,256]{1,0:T(8,128)(2,1)}, bf16[128,256]{1,0:T(8,128)(2,1)S(1)}, u32[]{:S(2)}, u32[]{:S(2)}) collective-permute-start(bf16[128,256]{1,0:T(8,128)(2,1)} %get-tuple-element.331), channel_id=1, source_target_pairs={{0,8},{8,16},{16,24},{24,32},{32,40},{40,48},{48,56},{56,64},{64,7... | collective-permute-start | bytes 196616 | tf_op jit(solution)/shard_map/while/body/eval_jaxpr/ppermute | solution.py:13
  122.3 8.3 %all-to-all-start = ((bf16[8,16,384]{2,1,0:T(8,128)(2,1)}), bf16[8,16,384]{2,1,0:T(8,128)(2,1)S(1)}, u32[]{:S(2)}, u32[]{:S(2)}) async-start(bf16[8,16,384]{2,1,0:T(8,128)(2,1)} %convert_element_type.88), calls=%async_computation | async-start | bytes 196608 | tf_op jit(solution)/shard_map/all_to_all | solution.py:76
  131.4 4.7 %all-to-all-done = bf16[8,16,384]{2,1,0:T(8,128)(2,1)S(1)} async-done(((bf16[8,16,384]{2,1,0:T(8,128)(2,1)}), bf16[8,16,384]{2,1,0:T(8,128)(2,1)S(1)}, u32[]{:S(2)}, u32[]{:S(2)}) %all-to-all-start) | async-done | bytes 98336 | tf_op jit(solution)/shard_map/all_to_all | solution.py:76
  139.1 13.7 %all_to_all.30 = bf16[8,6,3072]{2,1,0:T(8,128)(2,1)} all-to-all(bf16[8,6,3072]{2,1,0:T(8,128)(2,1)} %reshape.128), channel_id=1, replica_groups=mesh['ctx'=16,'exp'=8] {'exp'}, dimensions={0} | all-to-all | bytes 589824 | tf_op jit(solution)/shard_map/all_to_all | solution.py:95
  157.6 13.6 %all_to_all.31 = bf16[8,6,3072]{2,1,0:T(8,128)(2,1)} all-to-all(bf16[8,6,3072]{2,1,0:T(8,128)(2,1)} %reshape.132), channel_id=1, replica_groups=mesh['ctx'=16,'exp'=8] {'exp'}, dimensions={0} | all-to-all | bytes 589824 | tf_op jit(solution)/shard_map/all_to_all | solution.py:123
  173.1 48.4 %all-gather.3.cloned.1.call-done = bf16[768,3072]{1,0:T(8,128)(2,1)} async-done(((bf16[48,3072]{1,0:T(8,128)(2,1)}), bf16[768,3072]{1,0:T(8,128)(2,1)}) %all-gather.3.cloned.1.call-update) | async-done | bytes 4718608 | tf_op jit(solution)/shard_map/all_gather | solution.py:98
  221.5 7.2 %fusion.18 = f32[768,512]{1,0:T(8,128)} fusion(bf16[768,3072]{1,0:T(8,128)(2,1)} %all-gather.3.cloned.1.call-done, bf16[1,3072,512]{2,1,0:T(8,128)(2,1)} %param.20), kind=kOutput, calls=%fused_computation.33 | convolution fusion | flops 2415919104 | bytes 9437184 | tf_op jit(solution)/shard_map/dot_general | solution.py:103
  232.4 29.6 %all-gather.5.cloned.1.call-done = bf16[768,3072]{1,0:T(8,128)(2,1)} async-done(((bf16[48,3072]{1,0:T(8,128)(2,1)}), bf16[768,3072]{1,0:T(8,128)(2,1)}) %all-gather.5.cloned.1.call-update) | async-done | bytes 4718608 | tf_op jit(solution)/shard_map/all_gather | solution.py:127
  262.0 7.0 %multiply_convert_fusion = (bf16[768,512]{1,0:T(8,128)(2,1)}, bf16[768,512]{1,0:T(8,128)(2,1)}, bf16[768,512]{1,0:T(8,128)(2,1)S(1)}) fusion(f32[768,512]{1,0:T(8,128)} %fusion.22, f32[768,512]{1,0:T(8,128)} %fusion.18, bf16[768,3072]{1,0:T(8,128)(2,1)} %all-gather.5.cloned.1.call-done, bf16[1,512,3072]{2,1,0:T(8,128)(2,1)S(1)} %copy-done), kind=kOutput, calls=%fused_computation.39 | convolution fusion | flops 2421817344 | bytes 13369344 | tf_op jit(solution)/shard_map/dot_general | solution.py:130
  269.9 4.2 convolution_convert_fusion
  274.4 4.9 %fusion.20 = f32[768,3072]{1,0:T(8,128)S(1)} fusion(bf16[768,512]{1,0:T(8,128)(2,1)} %get-tuple-element.249, bf16[1,3072,512]{2,1,0:T(8,128)(2,1)} %param.19), kind=kOutput, calls=%fused_computation.35 | convolution fusion | flops 2415919104 | bytes 13369344 | tf_op jit(solution)/shard_map/dot_general | solution.py:147
  279.4 4.4 %add_convert_fusion = bf16[768,3072]{1,0:T(8,128)(2,1)} fusion(f32[768,3072]{1,0:T(8,128)S(1)} %fusion.20, bf16[768,512]{1,0:T(8,128)(2,1)S(1)} %copy-done.2, bf16[1,3072,512]{2,1,0:T(8,128)(2,1)S(1)} %copy-done.1), kind=kOutput, calls=%fused_computation.17 | convolution fusion | flops 2420637696 | bytes 18087936 | tf_op jit(solution)/shard_map/dot_general | solution.py:153
  283.8 6.9 %fusion.13 = bf16[1,512,3072]{2,1,0:T(8,128)(2,1)} fusion(bf16[768,512]{1,0:T(8,128)(2,1)} %copy-done.9, bf16[768,3072]{1,0:T(8,128)(2,1)} %all-gather.5.cloned.1.call-done), kind=kOutput, calls=%fused_computation.24 | convolution fusion | flops 2417491968 | bytes 8650752 | tf_op jit(solution)/shard_map/dot_general | solution.py:133
  290.7 51.4 %reduce-scatter.3.cloned.1.call-done = bf16[48,3072]{1,0:T(8,128)(2,1)} async-done(((bf16[768,3072]{1,0:T(8,128)(2,1)}), bf16[48,3072]{1,0:T(8,128)(2,1)}) %reduce-scatter.3.cloned.1.call-update) | async-done | bytes 294928 | tf_op jit(solution)/shard_map/reduce_scatter | solution.py:105
  343.9 7.5 %all-to-all-start.2 = ((bf16[8,6,3072]{2,1,0:T(8,128)(2,1)}), bf16[8,6,3072]{2,1,0:T(8,128)(2,1)}, u32[]{:S(2)}, u32[]{:S(2)}) async-start(bf16[8,6,3072]{2,1,0:T(8,128)(2,1)} %reshape.130), calls=%async_computation.3 | async-start | bytes 786432 | tf_op jit(solution)/shard_map/all_to_all | solution.py:111
  351.5 7.0 %fusion.12 = bf16[1,3072,512]{2,1,0:T(8,128)(2,1)} fusion(bf16[768,3072]{1,0:T(8,128)(2,1)} %all-gather.3.cloned.1.call-done, bf16[768,512]{1,0:T(8,128)(2,1)} %get-tuple-element.248), kind=kOutput, calls=%fused_computation.23 | convolution fusion | flops 2417491968 | bytes 8650752 | tf_op jit(solution)/shard_map/dot_general | solution.py:144
  358.5 52.4 %reduce-scatter.5.cloned.1.call-done = bf16[48,3072]{1,0:T(8,128)(2,1)} async-done(((bf16[768,3072]{1,0:T(8,128)(2,1)}), bf16[48,3072]{1,0:T(8,128)(2,1)}) %reduce-scatter.5.cloned.1.call-update) | async-done | bytes 294928 | tf_op jit(solution)/shard_map/reduce_scatter | solution.py:150
  412.7 7.5 %all-to-all-start.4 = ((bf16[8,6,3072]{2,1,0:T(8,128)(2,1)}), bf16[8,6,3072]{2,1,0:T(8,128)(2,1)}, u32[]{:S(2)}, u32[]{:S(2)}) async-start(bf16[8,6,3072]{2,1,0:T(8,128)(2,1)} %reshape.134), calls=%async_computation.6 | async-start | bytes 786432 | tf_op jit(solution)/shard_map/all_to_all | solution.py:161
  420.2 6.9 %fusion.11 = bf16[1,3072,512]{2,1,0:T(8,128)(2,1)} fusion(bf16[768,3072]{1,0:T(8,128)(2,1)} %all-gather.3.cloned.1.call-done, bf16[768,512]{1,0:T(8,128)(2,1)} %get-tuple-element.249), kind=kOutput, calls=%fused_computation.22 | convolution fusion | flops 2417491968 | bytes 8650752 | tf_op jit(solution)/shard_map/dot_general | solution.py:141
  (226 shorter events, 75.4 us)
Async XLA Ops:
  7.2 254.9 %copy-start = (bf16[1,512,3072]{2,1,0:T(8,128)(2,1)S(1)}, bf16[1,512,3072]{2,1,0:T(8,128)(2,1)}, u32[]{:S(2)}) copy-start(bf16[1,512,3072]{2,1,0:T(8,128)(2,1)} %param.21) | copy-start | bytes 9437188
  12.2 118.4 %copy-start.5 = (f32[16,2]{0,1:T(2,128)S(1)}, f32[16,2]{0,1:T(2,128)}, u32[]{:S(2)}) copy-start(f32[16,2]{0,1:T(2,128)} %param.17) | copy-start | bytes 388
  12.2 118.4 %copy-start.6 = (s32[16,2]{0,1:T(2,128)S(1)}, s32[16,2]{0,1:T(2,128)}, u32[]{:S(2)}) copy-start(s32[16,2]{0,1:T(2,128)} %param.16) | copy-start | bytes 388
  12.2 124.0 %copy-start.4 = (f32[3072]{0:T(1024)S(1)}, f32[3072]{0:T(1024)}, u32[]{:S(2)}) copy-start(f32[3072]{0:T(1024)} %param.15) | copy-start | bytes 36868
  12.2 2.8 collective-permute-start
  16.5 5.3 %collective-permute-start = (bf16[128,256]{1,0:T(8,128)(2,1)}, bf16[128,256]{1,0:T(8,128)(2,1)S(1)}, u32[]{:S(2)}, u32[]{:S(2)}) collective-permute-start(bf16[128,256]{1,0:T(8,128)(2,1)} %get-tuple-element.331), channel_id=1, source_target_pairs={{0,8},{8,16},{16,24},{24,32},{32,40},{40,48},{48,56},{56,64},{64,7... | collective-permute-start | bytes 196616 | tf_op jit(solution)/shard_map/while/body/eval_jaxpr/ppermute | solution.py:13
  23.3 5.8 %collective-permute-start = (bf16[128,256]{1,0:T(8,128)(2,1)}, bf16[128,256]{1,0:T(8,128)(2,1)S(1)}, u32[]{:S(2)}, u32[]{:S(2)}) collective-permute-start(bf16[128,256]{1,0:T(8,128)(2,1)} %get-tuple-element.331), channel_id=1, source_target_pairs={{0,8},{8,16},{16,24},{24,32},{32,40},{40,48},{48,56},{56,64},{64,7... | collective-permute-start | bytes 196616 | tf_op jit(solution)/shard_map/while/body/eval_jaxpr/ppermute | solution.py:13
  30.5 5.8 %collective-permute-start = (bf16[128,256]{1,0:T(8,128)(2,1)}, bf16[128,256]{1,0:T(8,128)(2,1)S(1)}, u32[]{:S(2)}, u32[]{:S(2)}) collective-permute-start(bf16[128,256]{1,0:T(8,128)(2,1)} %get-tuple-element.331), channel_id=1, source_target_pairs={{0,8},{8,16},{16,24},{24,32},{32,40},{40,48},{48,56},{56,64},{64,7... | collective-permute-start | bytes 196616 | tf_op jit(solution)/shard_map/while/body/eval_jaxpr/ppermute | solution.py:13
  37.8 5.8 %collective-permute-start = (bf16[128,256]{1,0:T(8,128)(2,1)}, bf16[128,256]{1,0:T(8,128)(2,1)S(1)}, u32[]{:S(2)}, u32[]{:S(2)}) collective-permute-start(bf16[128,256]{1,0:T(8,128)(2,1)} %get-tuple-element.331), channel_id=1, source_target_pairs={{0,8},{8,16},{16,24},{24,32},{32,40},{40,48},{48,56},{56,64},{64,7... | collective-permute-start | bytes 196616 | tf_op jit(solution)/shard_map/while/body/eval_jaxpr/ppermute | solution.py:13
  45.0 5.8 %collective-permute-start = (bf16[128,256]{1,0:T(8,128)(2,1)}, bf16[128,256]{1,0:T(8,128)(2,1)S(1)}, u32[]{:S(2)}, u32[]{:S(2)}) collective-permute-start(bf16[128,256]{1,0:T(8,128)(2,1)} %get-tuple-element.331), channel_id=1, source_target_pairs={{0,8},{8,16},{16,24},{24,32},{32,40},{40,48},{48,56},{56,64},{64,7... | collective-permute-start | bytes 196616 | tf_op jit(solution)/shard_map/while/body/eval_jaxpr/ppermute | solution.py:13
  52.3 5.8 %collective-permute-start = (bf16[128,256]{1,0:T(8,128)(2,1)}, bf16[128,256]{1,0:T(8,128)(2,1)S(1)}, u32[]{:S(2)}, u32[]{:S(2)}) collective-permute-start(bf16[128,256]{1,0:T(8,128)(2,1)} %get-tuple-element.331), channel_id=1, source_target_pairs={{0,8},{8,16},{16,24},{24,32},{32,40},{40,48},{48,56},{56,64},{64,7... | collective-permute-start | bytes 196616 | tf_op jit(solution)/shard_map/while/body/eval_jaxpr/ppermute | solution.py:13
  59.5 5.8 %collective-permute-start = (bf16[128,256]{1,0:T(8,128)(2,1)}, bf16[128,256]{1,0:T(8,128)(2,1)S(1)}, u32[]{:S(2)}, u32[]{:S(2)}) collective-permute-start(bf16[128,256]{1,0:T(8,128)(2,1)} %get-tuple-element.331), channel_id=1, source_target_pairs={{0,8},{8,16},{16,24},{24,32},{32,40},{40,48},{48,56},{56,64},{64,7... | collective-permute-start | bytes 196616 | tf_op jit(solution)/shard_map/while/body/eval_jaxpr/ppermute | solution.py:13
  66.7 5.8 %collective-permute-start = (bf16[128,256]{1,0:T(8,128)(2,1)}, bf16[128,256]{1,0:T(8,128)(2,1)S(1)}, u32[]{:S(2)}, u32[]{:S(2)}) collective-permute-start(bf16[128,256]{1,0:T(8,128)(2,1)} %get-tuple-element.331), channel_id=1, source_target_pairs={{0,8},{8,16},{16,24},{24,32},{32,40},{40,48},{48,56},{56,64},{64,7... | collective-permute-start | bytes 196616 | tf_op jit(solution)/shard_map/while/body/eval_jaxpr/ppermute | solution.py:13
  74.0 5.8 %collective-permute-start = (bf16[128,256]{1,0:T(8,128)(2,1)}, bf16[128,256]{1,0:T(8,128)(2,1)S(1)}, u32[]{:S(2)}, u32[]{:S(2)}) collective-permute-start(bf16[128,256]{1,0:T(8,128)(2,1)} %get-tuple-element.331), channel_id=1, source_target_pairs={{0,8},{8,16},{16,24},{24,32},{32,40},{40,48},{48,56},{56,64},{64,7... | collective-permute-start | bytes 196616 | tf_op jit(solution)/shard_map/while/body/eval_jaxpr/ppermute | solution.py:13
  81.2 5.8 %collective-permute-start = (bf16[128,256]{1,0:T(8,128)(2,1)}, bf16[128,256]{1,0:T(8,128)(2,1)S(1)}, u32[]{:S(2)}, u32[]{:S(2)}) collective-permute-start(bf16[128,256]{1,0:T(8,128)(2,1)} %get-tuple-element.331), channel_id=1, source_target_pairs={{0,8},{8,16},{16,24},{24,32},{32,40},{40,48},{48,56},{56,64},{64,7... | collective-permute-start | bytes 196616 | tf_op jit(solution)/shard_map/while/body/eval_jaxpr/ppermute | solution.py:13
  88.5 5.8 %collective-permute-start = (bf16[128,256]{1,0:T(8,128)(2,1)}, bf16[128,256]{1,0:T(8,128)(2,1)S(1)}, u32[]{:S(2)}, u32[]{:S(2)}) collective-permute-start(bf16[128,256]{1,0:T(8,128)(2,1)} %get-tuple-element.331), channel_id=1, source_target_pairs={{0,8},{8,16},{16,24},{24,32},{32,40},{40,48},{48,56},{56,64},{64,7... | collective-permute-start | bytes 196616 | tf_op jit(solution)/shard_map/while/body/eval_jaxpr/ppermute | solution.py:13
  95.7 5.8 %collective-permute-start = (bf16[128,256]{1,0:T(8,128)(2,1)}, bf16[128,256]{1,0:T(8,128)(2,1)S(1)}, u32[]{:S(2)}, u32[]{:S(2)}) collective-permute-start(bf16[128,256]{1,0:T(8,128)(2,1)} %get-tuple-element.331), channel_id=1, source_target_pairs={{0,8},{8,16},{16,24},{24,32},{32,40},{40,48},{48,56},{56,64},{64,7... | collective-permute-start | bytes 196616 | tf_op jit(solution)/shard_map/while/body/eval_jaxpr/ppermute | solution.py:13
  103.0 7.6 %collective-permute-start = (bf16[128,256]{1,0:T(8,128)(2,1)}, bf16[128,256]{1,0:T(8,128)(2,1)S(1)}, u32[]{:S(2)}, u32[]{:S(2)}) collective-permute-start(bf16[128,256]{1,0:T(8,128)(2,1)} %get-tuple-element.331), channel_id=1, source_target_pairs={{0,8},{8,16},{16,24},{24,32},{32,40},{40,48},{48,56},{56,64},{64,7... | collective-permute-start | bytes 196616 | tf_op jit(solution)/shard_map/while/body/eval_jaxpr/ppermute | solution.py:13
  112.0 7.9 %collective-permute-start = (bf16[128,256]{1,0:T(8,128)(2,1)}, bf16[128,256]{1,0:T(8,128)(2,1)S(1)}, u32[]{:S(2)}, u32[]{:S(2)}) collective-permute-start(bf16[128,256]{1,0:T(8,128)(2,1)} %get-tuple-element.331), channel_id=1, source_target_pairs={{0,8},{8,16},{16,24},{24,32},{32,40},{40,48},{48,56},{56,64},{64,7... | collective-permute-start | bytes 196616 | tf_op jit(solution)/shard_map/while/body/eval_jaxpr/ppermute | solution.py:13
  121.3 33.3 %copy-start.3 = (bf16[16,3072]{1,0:T(8,128)(2,1)S(1)}, bf16[16,3072]{1,0:T(8,128)(2,1)}, u32[]{:S(2)}) copy-start(bf16[16,3072]{1,0:T(8,128)(2,1)} %param.18) | copy-start | bytes 294916
  122.3 13.8 %all-to-all-start = ((bf16[8,16,384]{2,1,0:T(8,128)(2,1)}), bf16[8,16,384]{2,1,0:T(8,128)(2,1)S(1)}, u32[]{:S(2)}, u32[]{:S(2)}) async-start(bf16[8,16,384]{2,1,0:T(8,128)(2,1)} %convert_element_type.88), calls=%async_computation | async-start | bytes 196608 | tf_op jit(solution)/shard_map/all_to_all | solution.py:76
  130.6 90.9 %all-gather.3.cloned.1.call-start = ((), (), s32[]{:S(2)}) async-start(), calls=%async_computation.7 | async-start | bytes 5013504 | tf_op jit(solution)/shard_map/all_gather | solution.py:98
  154.6 107.4 %all-gather.5.cloned.1.call-start = ((), (), s32[]{:S(2)}) async-start(), calls=%async_computation.9 | async-start | bytes 5013504 | tf_op jit(solution)/shard_map/all_gather | solution.py:127
  173.0 169.0 %reduce-scatter.3.cloned.1.call-start = ((), (), s32[]{:S(2)}) async-start(), calls=%async_computation.8 | async-start | bytes 5013504 | tf_op jit(solution)/shard_map/reduce_scatter | solution.py:105
  221.5 7.2 %copy-start.7 = (bf16[768,3072]{1,0:T(8,128)(2,1)S(1)}, bf16[768,3072]{1,0:T(8,128)(2,1)}, u32[]{:S(2)}) copy-start(bf16[768,3072]{1,0:T(8,128)(2,1)} %all-gather.3.cloned.1.call-done) | copy-start | bytes 14155780
  221.5 7.2 %copy-start.8 = (bf16[1,3072,512]{2,1,0:T(8,128)(2,1)S(1)}, bf16[1,3072,512]{2,1,0:T(8,128)(2,1)}, u32[]{:S(2)}) copy-start(bf16[1,3072,512]{2,1,0:T(8,128)(2,1)} %param.19) | copy-start | bytes 9437188
  269.0 0.9 copy-start.9
  274.2 136.7 %reduce-scatter.5.cloned.1.call-start = ((), (), s32[]{:S(2)}) async-start(), calls=%async_computation.10 | async-start | bytes 5013504 | tf_op jit(solution)/shard_map/reduce_scatter | solution.py:150
  274.4 4.9 %copy-start.1 = (bf16[1,3072,512]{2,1,0:T(8,128)(2,1)S(1)}, bf16[1,3072,512]{2,1,0:T(8,128)(2,1)}, u32[]{:S(2)}) copy-start(bf16[1,3072,512]{2,1,0:T(8,128)(2,1)} %param.20) | copy-start | bytes 9437188
  274.4 4.9 %copy-start.2 = (bf16[768,512]{1,0:T(8,128)(2,1)S(1)}, bf16[768,512]{1,0:T(8,128)(2,1)}, u32[]{:S(2)}) copy-start(bf16[768,512]{1,0:T(8,128)(2,1)} %get-tuple-element.248) | copy-start | bytes 2359300
  343.9 68.8 %all-to-all-start.2 = ((bf16[8,6,3072]{2,1,0:T(8,128)(2,1)}), bf16[8,6,3072]{2,1,0:T(8,128)(2,1)}, u32[]{:S(2)}, u32[]{:S(2)}) async-start(bf16[8,6,3072]{2,1,0:T(8,128)(2,1)} %reshape.130), calls=%async_computation.3 | async-start | bytes 786432 | tf_op jit(solution)/shard_map/all_to_all | solution.py:111
  412.7 18.1 %all-to-all-start.4 = ((bf16[8,6,3072]{2,1,0:T(8,128)(2,1)}), bf16[8,6,3072]{2,1,0:T(8,128)(2,1)}, u32[]{:S(2)}, u32[]{:S(2)}) async-start(bf16[8,6,3072]{2,1,0:T(8,128)(2,1)} %reshape.134), calls=%async_computation.6 | async-start | bytes 786432 | tf_op jit(solution)/shard_map/all_to_all | solution.py:161
Sparse Core Ops, SparseCore 0:
  154.7 66.6 all-gather.2
  223.7 38.2 all-gather.4
  274.3 67.7 reduce-scatter.2
  344.4 66.4 reduce-scatter.4
where the time goes:
time: 443 us; the launch traced here: 441 us
  waiting for transfers between devices  202 us (46%)
  starting transfers between devices  94.5 us (21%)
  matrix products  69.6 us (16%)
  local copies, waits for them, and re-layouts  27.4 us (6%)
  blocking collectives  27.3 us (6%)
  between operations  14 us (3%)
  other arithmetic  5.04 us (1%)
    ppermute x15, starting transfers between devices, shifted(): return lax.ppermute(block, axis, route)  70.9 us
    reduce_scatter x1, waiting for transfers between devices, local(): lax.psum_scatter((term + lax.dot_general(grad_up_pre, up_w, (((1,), (1,))...  52.4 us
    reduce_scatter x1, waiting for transfers between devices, local(): lax.psum_scatter(jnp.dot(hidden, down_w, preferred_element_type=jnp.float...  51.4 us
    all_gather x1, waiting for transfers between devices, local(): expert_in = lax.all_gather(arrived, 'ctx', axis=0, tiled=True)  48.4 us
    all_gather x1, waiting for transfers between devices, local(): lax.all_gather(grad_arrived, 'ctx', axis=0, tiled=True)  29.6 us
    ppermute x15, waiting for transfers between devices, shifted(): return lax.ppermute(block, axis, route)  15.6 us
    all_to_all x1, blocking collectives, local(): lax.all_to_all(send.reshape(n_exp, capacity, width), 'exp', split_axis=0,...  13.7 us
    all_to_all x1, blocking collectives, local(): lax.all_to_all(grad_slots.reshape(n_exp, capacity, width), 'exp', split_a...  13.6 us
  transfers between devices with their start and end apart: 22, of which 20 were waited for; matrix products, arithmetic and copies ran while one was open for 12% of the time, Pallas kernels for 0%

commit v1 on v0

--- a/solution.py
+++ b/solution.py
@@ -5,6 +5,11 @@
 
 norm_eps = 1e-05
 masked_value = -1e30
+
+
+def gather_over(block, axis, d):
+    repeated = jnp.stack([block] * lax.axis_size(axis))
+    return jnp.concatenate(lax.all_to_all(repeated, axis, 0, 0), axis=d)
 
 
 def shifted(block, axis, distance):
@@ -95,7 +100,7 @@
     arrived = lax.all_to_all(
         send.reshape(n_exp, capacity, width), "exp", split_axis=0, concat_axis=0, tiled=True
     ).reshape(slots, width)
-    expert_in = lax.all_gather(arrived, "ctx", axis=0, tiled=True)
+    expert_in = gather_over(arrived, "ctx", 0)
     gate_w = w_gate[0]
     up_w = w_up[0]
     down_w = w_down[0]

time: 443 us -> 484 us (1.093)
  blocking collectives: 27.3 us -> 134 us
  waiting for transfers between devices: 202 us -> 120 us
  matrix products: 69.6 us -> 78.7 us
  other arithmetic: 5.04 us -> 10.2 us
    all_to_all x1 -> x2, blocking collectives: 13.6 us -> 120 us  [the longest x1 109 us: gather_over(): return jnp.concatenate(lax.all_to_all(repeated, axis, 0, 0), axis=d)]
    all_gather x1, waiting for transfers between devices: 48.4 us -> 0.01 us  [local(): lax.all_gather(arrived, 'ctx', axis=0, tiled=True)]
    all_gather x1, waiting for transfers between devices: 29.6 us -> 0.01 us  [local(): lax.all_gather(grad_arrived, 'ctx', axis=0, tiled=True)]
    dot_general x16, matrix products: 4 us -> 17.4 us  [attend_piece(): lax.dot_general(query_flat, key_part, (((1,), (1,)), ((), ())), preferred...]
    reduce_scatter x1, waiting for transfers between devices: 52.4 us -> 47.4 us  [local(): lax.psum_scatter((term + lax.dot_general(grad_up_pre, up_w, (((1,), (1,))...]
  transfers between devices with their start and end apart: 22 -> 22, of which waited for: 20 -> 19; matrix products, arithmetic and copies ran while one was open for 12% -> 21% of each run, Pallas kernels for 0% -> 0%
where the time goes in v1:
time: 484 us; the launch traced here: 479 us
  blocking collectives  134 us (28%)
  waiting for transfers between devices  120 us (25%)
  starting transfers between devices  94.5 us (20%)
  matrix products  78.7 us (16%)
  local copies, waits for them, and re-layouts  27.1 us (6%)
  between operations  14 us (3%)
  other arithmetic  10.2 us (2%)
    all_to_all x1, blocking collectives, gather_over(): return jnp.concatenate(lax.all_to_all(repeated, axis, 0, 0), axis=d)  109 us
    ppermute x15, starting transfers between devices, shifted(): return lax.ppermute(block, axis, route)  71.1 us
    reduce_scatter x1, waiting for transfers between devices, local(): lax.psum_scatter(jnp.dot(hidden, down_w, preferred_element_type=jnp.float...  52.5 us
    reduce_scatter x1, waiting for transfers between devices, local(): lax.psum_scatter((term + lax.dot_general(grad_up_pre, up_w, (((1,), (1,))...  47.4 us
    dot_general x16, matrix products, attend_piece(): lax.dot_general(query_flat, key_part, (((1,), (1,)), ((), ())), preferred...  17.4 us
    ppermute x15, waiting for transfers between devices, shifted(): return lax.ppermute(block, axis, route)  15.6 us
    all_to_all x1, blocking collectives, local(): lax.all_to_all(send.reshape(n_exp, capacity, width), 'exp', split_axis=0,...  13.6 us
    all_to_all x1, blocking collectives, local(): lax.all_to_all(attended, 'exp', split_axis=0, concat_axis=1, tiled=True)  10.9 us
  transfers between devices with their start and end apart: 22, of which 19 were waited for; matrix products, arithmetic and copies ran while one was open for 21% of the time, Pallas kernels for 0%

profile of v1, /device:TPU:16, one launch (start us, length us, event | category | flops | bytes accessed | tf_op | source)
XLA Modules:
  0.0 479.3 jit_solution(10778050658558806661)
XLA Ops:
  13.7 8.3 %all-to-all-start.4 = ((bf16[8,6,3072]{2,1,0:T(8,128)(2,1)}), bf16[8,6,3072]{2,1,0:T(8,128)(2,1)}, u32[]{:S(2)}, u32[]{:S(2)}) async-start(bf16[8,6,3072]{2,1,0:T(8,128)(2,1)} %reshape.135), calls=%async_computation.5 | async-start | bytes 786432 | tf_op jit(solution)/shard_map/all_to_all | solution.py:128
  31.2 122.7 %while.22 = (s32[]{:T(128)}, f32[384]{0:T(512)S(1)}, f32[384]{0:T(512)S(1)}, f32[384,128]{1,0:T(8,128)S(1)}, bf16[128,256]{1,0:T(8,128)(2,1)}, /*index=5*/s32[]{...) while((s32[]{:T(128)}, f32[384]{0:T(512)S(1)}, ...), condition=%wide.region_11.12_spmd.clone, body=%wide.region_8.11_spmd.clone.sunk | while | flops 88720656 | bytes 1575218 | solution.py:72
  36.0 4.7 collective-permute-start
  44.1 5.8 %collective-permute-start = (bf16[128,256]{1,0:T(8,128)(2,1)}, bf16[128,256]{1,0:T(8,128)(2,1)S(1)}, u32[]{:S(2)}, u32[]{:S(2)}) collective-permute-start(bf16[128,256]{1,0:T(8,128)(2,1)} %get-tuple-element.331), channel_id=1, source_target_pairs={{0,8},{8,16},{16,24},{24,32},{32,40},{40,48},{48,56},{56,64},{64,7... | collective-permute-start | bytes 196616 | tf_op jit(solution)/shard_map/while/body/eval_jaxpr/ppermute | solution.py:18
  53.3 6.1 %collective-permute-start = (bf16[128,256]{1,0:T(8,128)(2,1)}, bf16[128,256]{1,0:T(8,128)(2,1)S(1)}, u32[]{:S(2)}, u32[]{:S(2)}) collective-permute-start(bf16[128,256]{1,0:T(8,128)(2,1)} %get-tuple-element.331), channel_id=1, source_target_pairs={{0,8},{8,16},{16,24},{24,32},{32,40},{40,48},{48,56},{56,64},{64,7... | collective-permute-start | bytes 196616 | tf_op jit(solution)/shard_map/while/body/eval_jaxpr/ppermute | solution.py:18
  62.8 5.7 %collective-permute-start = (bf16[128,256]{1,0:T(8,128)(2,1)}, bf16[128,256]{1,0:T(8,128)(2,1)S(1)}, u32[]{:S(2)}, u32[]{:S(2)}) collective-permute-start(bf16[128,256]{1,0:T(8,128)(2,1)} %get-tuple-element.331), channel_id=1, source_target_pairs={{0,8},{8,16},{16,24},{24,32},{32,40},{40,48},{48,56},{56,64},{64,7... | collective-permute-start | bytes 196616 | tf_op jit(solution)/shard_map/while/body/eval_jaxpr/ppermute | solution.py:18
  72.0 4.8 %collective-permute-start = (bf16[128,256]{1,0:T(8,128)(2,1)}, bf16[128,256]{1,0:T(8,128)(2,1)S(1)}, u32[]{:S(2)}, u32[]{:S(2)}) collective-permute-start(bf16[128,256]{1,0:T(8,128)(2,1)} %get-tuple-element.331), channel_id=1, source_target_pairs={{0,8},{8,16},{16,24},{24,32},{32,40},{40,48},{48,56},{56,64},{64,7... | collective-permute-start | bytes 196616 | tf_op jit(solution)/shard_map/while/body/eval_jaxpr/ppermute | solution.py:18
  80.2 4.7 collective-permute-start
  88.4 4.7 collective-permute-start
  96.5 4.7 collective-permute-start
  104.6 4.7 collective-permute-start
  112.8 4.7 collective-permute-start
  120.9 4.7 collective-permute-start
  129.1 4.7 collective-permute-start
  137.2 4.7 collective-permute-start
  145.3 5.1 %collective-permute-start = (bf16[128,256]{1,0:T(8,128)(2,1)}, bf16[128,256]{1,0:T(8,128)(2,1)S(1)}, u32[]{:S(2)}, u32[]{:S(2)}) collective-permute-start(bf16[128,256]{1,0:T(8,128)(2,1)} %get-tuple-element.331), channel_id=1, source_target_pairs={{0,8},{8,16},{16,24},{24,32},{32,40},{40,48},{48,56},{56,64},{64,7... | collective-permute-start | bytes 196616 | tf_op jit(solution)/shard_map/while/body/eval_jaxpr/ppermute | solution.py:18
  154.2 10.9 %all_to_all.35 = bf16[8,16,384]{2,1,0:T(8,128)(2,1)S(1)} all-to-all(bf16[8,16,384]{2,1,0:T(8,128)(2,1)S(1)} %convert_element_type.88), channel_id=1, replica_groups=mesh['ctx'=16,'exp'=8] {'exp'}, dimensions={0} | all-to-all | bytes 196608 | tf_op jit(solution)/shard_map/all_to_all | solution.py:81
  168.1 13.6 %all_to_all.36 = bf16[8,6,3072]{2,1,0:T(8,128)(2,1)} all-to-all(bf16[8,6,3072]{2,1,0:T(8,128)(2,1)} %reshape.131), channel_id=1, replica_groups=mesh['ctx'=16,'exp'=8] {'exp'}, dimensions={0} | all-to-all | bytes 589824 | tf_op jit(solution)/shard_map/all_to_all | solution.py:100
  185.2 109.3 %all_to_all.37 = bf16[16,48,3072]{2,1,0:T(8,128)(2,1)S(1)} all-to-all(bf16[16,48,3072]{2,1,0:T(8,128)(2,1)S(1)} %stack.3), channel_id=1, replica_groups=mesh['ctx'=16,'exp'=8] {'ctx'}, dimensions={0} | all-to-all | bytes 9437184 | tf_op jit(solution)/shard_map/all_to_all | solution.py:12
  294.5 3.7 fusion.18
  298.2 3.7 fusion.22
  302.0 7.0 %multiply_convert_fusion = (bf16[768,512]{1,0:T(8,128)(2,1)S(1)}, bf16[768,512]{1,0:T(8,128)(2,1)S(1)}, bf16[768,512]{1,0:T(8,128)(2,1)}) fusion(f32[768,512]{1,0:T(8,128)} %fusion.22, f32[768,512]{1,0:T(8,128)} %fusion.18, bf16[768,3072]{1,0:T(8,128)(2,1)} %all-gather.3.cloned.1.call-done, bf16[1,512,3072]{2,1,0:T(8,128)(2,1)S(1)} %copy-done), kind=kOutput, calls=%fused_computation.39 | convolution fusion | flops 2421817344 | bytes 13369344 | tf_op jit(solution)/shard_map/dot_general | solution.py:135
  311.7 4.5 add_convert_fusion
  316.4 5.4 %convolution_convert_fusion = bf16[768,3072]{1,0:T(8,128)(2,1)} fusion(bf16[768,512]{1,0:T(8,128)(2,1)} %get-tuple-element.250, bf16[1,512,3072]{2,1,0:T(8,128)(2,1)S(1)} %copy-done), kind=kOutput, calls=%fused_computation.18 | convolution fusion | flops 2418278400 | bytes 8650752 | tf_op jit(solution)/shard_map/dot_general | solution.py:111
  321.9 6.9 %fusion.13 = bf16[1,512,3072]{2,1,0:T(8,128)(2,1)} fusion(bf16[768,512]{1,0:T(8,128)(2,1)} %get-tuple-element.250, bf16[768,3072]{1,0:T(8,128)(2,1)} %all-gather.3.cloned.1.call-done), kind=kOutput, calls=%fused_computation.24 | convolution fusion | flops 2417491968 | bytes 8650752 | tf_op jit(solution)/shard_map/dot_general | solution.py:138
  328.8 7.0 %fusion.11 = bf16[1,3072,512]{2,1,0:T(8,128)(2,1)} fusion(bf16[768,3072]{1,0:T(8,128)(2,1)} %all-gather.5.cloned.1.call-done, bf16[768,512]{1,0:T(8,128)(2,1)} %copy-done.14), kind=kOutput, calls=%fused_computation.22 | convolution fusion | flops 2417491968 | bytes 8650752 | tf_op jit(solution)/shard_map/dot_general | solution.py:146
  335.8 47.4 %reduce-scatter.5.cloned.1.call-done = bf16[48,3072]{1,0:T(8,128)(2,1)} async-done(((bf16[768,3072]{1,0:T(8,128)(2,1)}), bf16[48,3072]{1,0:T(8,128)(2,1)}) %reduce-scatter.5.cloned.1.call-update) | async-done | bytes 294928 | tf_op jit(solution)/shard_map/reduce_scatter | solution.py:155
  385.0 7.4 %all-to-all-start.5 = ((bf16[8,6,3072]{2,1,0:T(8,128)(2,1)}), bf16[8,6,3072]{2,1,0:T(8,128)(2,1)}, u32[]{:S(2)}, u32[]{:S(2)}) async-start(bf16[8,6,3072]{2,1,0:T(8,128)(2,1)} %reshape.137), calls=%async_computation.7 | async-start | bytes 786432 | tf_op jit(solution)/shard_map/all_to_all | solution.py:166
  392.4 7.0 %fusion.12 = bf16[1,3072,512]{2,1,0:T(8,128)(2,1)} fusion(bf16[768,3072]{1,0:T(8,128)(2,1)} %all-gather.5.cloned.1.call-done, bf16[768,512]{1,0:T(8,128)(2,1)} %copy-done.3), kind=kOutput, calls=%fused_computation.23 | convolution fusion | flops 2417491968 | bytes 8650752 | tf_op jit(solution)/shard_map/dot_general | solution.py:149
  399.4 52.5 %reduce-scatter.3.cloned.1.call-done = bf16[48,3072]{1,0:T(8,128)(2,1)} async-done(((bf16[768,3072]{1,0:T(8,128)(2,1)}), bf16[48,3072]{1,0:T(8,128)(2,1)}) %reduce-scatter.3.cloned.1.call-update) | async-done | bytes 294928 | tf_op jit(solution)/shard_map/reduce_scatter | solution.py:110
  453.8 7.4 %all-to-all-start.3 = ((bf16[8,6,3072]{2,1,0:T(8,128)(2,1)}), bf16[8,6,3072]{2,1,0:T(8,128)(2,1)}, u32[]{:S(2)}, u32[]{:S(2)}) async-start(bf16[8,6,3072]{2,1,0:T(8,128)(2,1)} %reshape.133), calls=%async_computation.4 | async-start | bytes 786432 | tf_op jit(solution)/shard_map/all_to_all | solution.py:116
  465.0 2.8 all-to-all-done.3
  (238 shorter events, 89.3 us)
Async XLA Ops:
  7.2 294.8 %copy-start = (bf16[1,512,3072]{2,1,0:T(8,128)(2,1)S(1)}, bf16[1,512,3072]{2,1,0:T(8,128)(2,1)}, u32[]{:S(2)}) copy-start(bf16[1,512,3072]{2,1,0:T(8,128)(2,1)} %param.21) | copy-start | bytes 9437188
  11.5 11.7 %copy-start.5 = (f32[48,16]{0,1:T(8,128)}, f32[48,16]{0,1:T(8,128)S(1)}, u32[]{:S(2)}) copy-start(f32[48,16]{0,1:T(8,128)S(1)} %get-tuple-element.227) | copy-start | bytes 9220
  13.7 15.6 %all-to-all-start.4 = ((bf16[8,6,3072]{2,1,0:T(8,128)(2,1)}), bf16[8,6,3072]{2,1,0:T(8,128)(2,1)}, u32[]{:S(2)}, u32[]{:S(2)}) async-start(bf16[8,6,3072]{2,1,0:T(8,128)(2,1)} %reshape.135), calls=%async_computation.5 | async-start | bytes 786432 | tf_op jit(solution)/shard_map/all_to_all | solution.py:128
  22.0 280.0 %all-gather.3.cloned.1.call-start = ((), (), s32[]{:S(2)}) async-start(), calls=%async_computation.9 | async-start | bytes 5013504 | tf_op jit(solution)/shard_map/all_gather | solution.py:132
  23.2 3.8 copy-start.4
  31.2 297.7 %all-gather.5.cloned.1.call-start = ((), (), s32[]{:S(2)}) async-start(), calls=%async_computation.11 | async-start | bytes 5013504 | tf_op jit(solution)/shard_map/all_gather | solution.py:133
  31.2 134.1 %copy-start.7 = (f32[3072]{0:T(1024)S(1)}, f32[3072]{0:T(1024)}, u32[]{:S(2)}) copy-start(f32[3072]{0:T(1024)} %param.15) | copy-start | bytes 36868
  31.2 2.4 collective-permute-start
  36.0 5.8 %collective-permute-start = (bf16[128,256]{1,0:T(8,128)(2,1)}, bf16[128,256]{1,0:T(8,128)(2,1)S(1)}, u32[]{:S(2)}, u32[]{:S(2)}) collective-permute-start(bf16[128,256]{1,0:T(8,128)(2,1)} %get-tuple-element.331), channel_id=1, source_target_pairs={{0,8},{8,16},{16,24},{24,32},{32,40},{40,48},{48,56},{56,64},{64,7... | collective-permute-start | bytes 196616 | tf_op jit(solution)/shard_map/while/body/eval_jaxpr/ppermute | solution.py:18
  44.1 6.9 %collective-permute-start = (bf16[128,256]{1,0:T(8,128)(2,1)}, bf16[128,256]{1,0:T(8,128)(2,1)S(1)}, u32[]{:S(2)}, u32[]{:S(2)}) collective-permute-start(bf16[128,256]{1,0:T(8,128)(2,1)} %get-tuple-element.331), channel_id=1, source_target_pairs={{0,8},{8,16},{16,24},{24,32},{32,40},{40,48},{48,56},{56,64},{64,7... | collective-permute-start | bytes 196616 | tf_op jit(solution)/shard_map/while/body/eval_jaxpr/ppermute | solution.py:18
  53.3 7.2 %collective-permute-start = (bf16[128,256]{1,0:T(8,128)(2,1)}, bf16[128,256]{1,0:T(8,128)(2,1)S(1)}, u32[]{:S(2)}, u32[]{:S(2)}) collective-permute-start(bf16[128,256]{1,0:T(8,128)(2,1)} %get-tuple-element.331), channel_id=1, source_target_pairs={{0,8},{8,16},{16,24},{24,32},{32,40},{40,48},{48,56},{56,64},{64,7... | collective-permute-start | bytes 196616 | tf_op jit(solution)/shard_map/while/body/eval_jaxpr/ppermute | solution.py:18
  62.8 6.8 %collective-permute-start = (bf16[128,256]{1,0:T(8,128)(2,1)}, bf16[128,256]{1,0:T(8,128)(2,1)S(1)}, u32[]{:S(2)}, u32[]{:S(2)}) collective-permute-start(bf16[128,256]{1,0:T(8,128)(2,1)} %get-tuple-element.331), channel_id=1, source_target_pairs={{0,8},{8,16},{16,24},{24,32},{32,40},{40,48},{48,56},{56,64},{64,7... | collective-permute-start | bytes 196616 | tf_op jit(solution)/shard_map/while/body/eval_jaxpr/ppermute | solution.py:18
  72.0 5.9 %collective-permute-start = (bf16[128,256]{1,0:T(8,128)(2,1)}, bf16[128,256]{1,0:T(8,128)(2,1)S(1)}, u32[]{:S(2)}, u32[]{:S(2)}) collective-permute-start(bf16[128,256]{1,0:T(8,128)(2,1)} %get-tuple-element.331), channel_id=1, source_target_pairs={{0,8},{8,16},{16,24},{24,32},{32,40},{40,48},{48,56},{56,64},{64,7... | collective-permute-start | bytes 196616 | tf_op jit(solution)/shard_map/while/body/eval_jaxpr/ppermute | solution.py:18
  80.2 5.8 %collective-permute-start = (bf16[128,256]{1,0:T(8,128)(2,1)}, bf16[128,256]{1,0:T(8,128)(2,1)S(1)}, u32[]{:S(2)}, u32[]{:S(2)}) collective-permute-start(bf16[128,256]{1,0:T(8,128)(2,1)} %get-tuple-element.331), channel_id=1, source_target_pairs={{0,8},{8,16},{16,24},{24,32},{32,40},{40,48},{48,56},{56,64},{64,7... | collective-permute-start | bytes 196616 | tf_op jit(solution)/shard_map/while/body/eval_jaxpr/ppermute | solution.py:18
  88.4 5.8 %collective-permute-start = (bf16[128,256]{1,0:T(8,128)(2,1)}, bf16[128,256]{1,0:T(8,128)(2,1)S(1)}, u32[]{:S(2)}, u32[]{:S(2)}) collective-permute-start(bf16[128,256]{1,0:T(8,128)(2,1)} %get-tuple-element.331), channel_id=1, source_target_pairs={{0,8},{8,16},{16,24},{24,32},{32,40},{40,48},{48,56},{56,64},{64,7... | collective-permute-start | bytes 196616 | tf_op jit(solution)/shard_map/while/body/eval_jaxpr/ppermute | solution.py:18
  96.5 5.8 %collective-permute-start = (bf16[128,256]{1,0:T(8,128)(2,1)}, bf16[128,256]{1,0:T(8,128)(2,1)S(1)}, u32[]{:S(2)}, u32[]{:S(2)}) collective-permute-start(bf16[128,256]{1,0:T(8,128)(2,1)} %get-tuple-element.331), channel_id=1, source_target_pairs={{0,8},{8,16},{16,24},{24,32},{32,40},{40,48},{48,56},{56,64},{64,7... | collective-permute-start | bytes 196616 | tf_op jit(solution)/shard_map/while/body/eval_jaxpr/ppermute | solution.py:18
  104.6 5.8 %collective-permute-start = (bf16[128,256]{1,0:T(8,128)(2,1)}, bf16[128,256]{1,0:T(8,128)(2,1)S(1)}, u32[]{:S(2)}, u32[]{:S(2)}) collective-permute-start(bf16[128,256]{1,0:T(8,128)(2,1)} %get-tuple-element.331), channel_id=1, source_target_pairs={{0,8},{8,16},{16,24},{24,32},{32,40},{40,48},{48,56},{56,64},{64,7... | collective-permute-start | bytes 196616 | tf_op jit(solution)/shard_map/while/body/eval_jaxpr/ppermute | solution.py:18
  112.8 5.8 %collective-permute-start = (bf16[128,256]{1,0:T(8,128)(2,1)}, bf16[128,256]{1,0:T(8,128)(2,1)S(1)}, u32[]{:S(2)}, u32[]{:S(2)}) collective-permute-start(bf16[128,256]{1,0:T(8,128)(2,1)} %get-tuple-element.331), channel_id=1, source_target_pairs={{0,8},{8,16},{16,24},{24,32},{32,40},{40,48},{48,56},{56,64},{64,7... | collective-permute-start | bytes 196616 | tf_op jit(solution)/shard_map/while/body/eval_jaxpr/ppermute | solution.py:18
  120.9 5.8 %collective-permute-start = (bf16[128,256]{1,0:T(8,128)(2,1)}, bf16[128,256]{1,0:T(8,128)(2,1)S(1)}, u32[]{:S(2)}, u32[]{:S(2)}) collective-permute-start(bf16[128,256]{1,0:T(8,128)(2,1)} %get-tuple-element.331), channel_id=1, source_target_pairs={{0,8},{8,16},{16,24},{24,32},{32,40},{40,48},{48,56},{56,64},{64,7... | collective-permute-start | bytes 196616 | tf_op jit(solution)/shard_map/while/body/eval_jaxpr/ppermute | solution.py:18
  129.1 5.8 %collective-permute-start = (bf16[128,256]{1,0:T(8,128)(2,1)}, bf16[128,256]{1,0:T(8,128)(2,1)S(1)}, u32[]{:S(2)}, u32[]{:S(2)}) collective-permute-start(bf16[128,256]{1,0:T(8,128)(2,1)} %get-tuple-element.331), channel_id=1, source_target_pairs={{0,8},{8,16},{16,24},{24,32},{32,40},{40,48},{48,56},{56,64},{64,7... | collective-permute-start | bytes 196616 | tf_op jit(solution)/shard_map/while/body/eval_jaxpr/ppermute | solution.py:18
  137.2 5.8 %collective-permute-start = (bf16[128,256]{1,0:T(8,128)(2,1)}, bf16[128,256]{1,0:T(8,128)(2,1)S(1)}, u32[]{:S(2)}, u32[]{:S(2)}) collective-permute-start(bf16[128,256]{1,0:T(8,128)(2,1)} %get-tuple-element.331), channel_id=1, source_target_pairs={{0,8},{8,16},{16,24},{24,32},{32,40},{40,48},{48,56},{56,64},{64,7... | collective-permute-start | bytes 196616 | tf_op jit(solution)/shard_map/while/body/eval_jaxpr/ppermute | solution.py:18
  145.3 6.2 %collective-permute-start = (bf16[128,256]{1,0:T(8,128)(2,1)}, bf16[128,256]{1,0:T(8,128)(2,1)S(1)}, u32[]{:S(2)}, u32[]{:S(2)}) collective-permute-start(bf16[128,256]{1,0:T(8,128)(2,1)} %get-tuple-element.331), channel_id=1, source_target_pairs={{0,8},{8,16},{16,24},{24,32},{32,40},{40,48},{48,56},{56,64},{64,7... | collective-permute-start | bytes 196616 | tf_op jit(solution)/shard_map/while/body/eval_jaxpr/ppermute | solution.py:18
  165.3 19.9 %copy-start.11 = (f32[16]{0:T(128)}, f32[16]{0:T(128)S(1)}, u32[]{:S(2)}) copy-start(f32[16]{0:T(128)S(1)} %fusion.26) | copy-start | bytes 196
  165.3 19.9 %copy-start.10 = (f32[16]{0:T(128)}, f32[16]{0:T(128)S(1)}, u32[]{:S(2)}) copy-start(f32[16]{0:T(128)S(1)} %add_rsqrt_fusion) | copy-start | bytes 196
  183.6 199.6 %reduce-scatter.5.cloned.1.call-start = ((), (), s32[]{:S(2)}) async-start(), calls=%async_computation.10 | async-start | bytes 5013504 | tf_op jit(solution)/shard_map/reduce_scatter | solution.py:155
  185.2 109.3 %copy-start.1 = (bf16[1,3072,512]{2,1,0:T(8,128)(2,1)S(1)}, bf16[1,3072,512]{2,1,0:T(8,128)(2,1)}, u32[]{:S(2)}) copy-start(bf16[1,3072,512]{2,1,0:T(8,128)(2,1)} %param.20) | copy-start | bytes 9437188
  294.5 3.7 copy-start.12
  302.0 7.0 %copy-start.13 = (bf16[1,3072,512]{2,1,0:T(8,128)(2,1)S(1)}, bf16[1,3072,512]{2,1,0:T(8,128)(2,1)}, u32[]{:S(2)}) copy-start(bf16[1,3072,512]{2,1,0:T(8,128)(2,1)} %param.19) | copy-start | bytes 9437188
  316.2 135.8 %reduce-scatter.3.cloned.1.call-start = ((), (), s32[]{:S(2)}) async-start(), calls=%async_computation.8 | async-start | bytes 5013504 | tf_op jit(solution)/shard_map/reduce_scatter | solution.py:110
  385.0 68.8 %all-to-all-start.5 = ((bf16[8,6,3072]{2,1,0:T(8,128)(2,1)}), bf16[8,6,3072]{2,1,0:T(8,128)(2,1)}, u32[]{:S(2)}, u32[]{:S(2)}) async-start(bf16[8,6,3072]{2,1,0:T(8,128)(2,1)} %reshape.137), calls=%async_computation.7 | async-start | bytes 786432 | tf_op jit(solution)/shard_map/all_to_all | solution.py:166
  399.4 70.2 %copy-start.6 = (f32[48,16]{0,1:T(8,128)S(1)}, f32[48,16]{0,1:T(8,128)}, u32[]{:S(2)}) copy-start(f32[48,16]{0,1:T(8,128)} %copy-done.5) | copy-start | bytes 9220
  453.8 14.1 %all-to-all-start.3 = ((bf16[8,6,3072]{2,1,0:T(8,128)(2,1)}), bf16[8,6,3072]{2,1,0:T(8,128)(2,1)}, u32[]{:S(2)}, u32[]{:S(2)}) async-start(bf16[8,6,3072]{2,1,0:T(8,128)(2,1)} %reshape.133), calls=%async_computation.4 | async-start | bytes 786432 | tf_op jit(solution)/shard_map/all_to_all | solution.py:116
  (5 other events, 12.4 us)
Sparse Core Ops, SparseCore 0:
  31.3 38.4 all-gather.2
  183.7 112.9 all-gather.4
  316.3 66.8 reduce-scatter.4
  385.5 66.4 reduce-scatter.2
